TPU v7x, 32 devices: a whole 2x2x4 slice. The times are simulated.
32 devices in a mesh: grp: 8 (over z, y), tm: 4 (over x, core).
Axes of the slice: x: 2, y: 2, z: 4, core: 2. Of those that a mesh axis runs over, the one named last changes fastest.
Arguments:
- voltages: bfloat16 [1024, 12, 16384], P('grp', 'tm'), may hold values from -6 to 6
Outputs:
- visibilities: float32 [2, 128, 1024, 1024], P(None, 'grp', 'tm')
All inputs are finite; a program needn't handle non-finite values.
Results may differ from a plain program's by a relative error of at most 0.0053.
Values may be sent and summed in bfloat16 or wider, within the bound.
A program may use at most 192 MiB of HBM per device.

v0:
```python
import math

import jax
import jax.numpy as jnp
from jax import lax
from jax.sharding import PartitionSpec as P

CH = 128
TAPS = 4
FIRST = 2048


def shifted(x, axis, by):
    length = lax.axis_size(axis)
    pairs = [(i, i + by) for i in range(length) if 0 <= i + by < length]
    return lax.ppermute(x, axis, pairs)


def tap_table(frame_len, channels, first_bin, tap_count):
    sample = jnp.arange(frame_len, dtype=jnp.int32)
    channel = first_bin + jnp.arange(channels, dtype=jnp.int32)
    phase_index = sample[:, None] * channel[None, :] % frame_len
    angles = phase_index.astype(jnp.float32) * jnp.float32(2.0 * math.pi / frame_len)
    cosine = jnp.cos(angles)
    sine_vals = jnp.sin(angles)
    columns = []
    for tap_idx in range(tap_count):
        offset = ((tap_count - 1 - tap_idx) * frame_len + sample).astype(jnp.float32) + 0.5
        argument = offset / frame_len - tap_count / 2.0
        shape_part = jnp.sin(math.pi * argument) / (math.pi * argument)
        window = shape_part * (
            0.5 - 0.5 * jnp.cos(offset * jnp.float32(2.0 * math.pi / (tap_count * frame_len)))
        )
        scaled = window[:, None] * frame_len ** (-0.5)
        columns.append(scaled * cosine)
        columns.append(-scaled * sine_vals)
    return jnp.concatenate(columns, axis=1).astype(jnp.bfloat16)


def carry_terms(tail_taps, warmup):
    result = jnp.zeros((tail_taps.shape[0], warmup, tail_taps.shape[3]), jnp.float32)
    for tap_idx in range(1, warmup + 1):
        result = result + jnp.pad(
            tail_taps[:, warmup - tap_idx :, tap_idx, :], ((0, 0), (0, warmup - tap_idx), (0, 0))
        )
    return result


def cross_terms(segment, row_start, row_count):
    row_part = lax.dynamic_slice_in_dim(segment, row_start, row_count, 3)
    real_sum = jnp.einsum(
        "scr,scn->crn", row_part[0], segment[0], preferred_element_type=jnp.float32
    )
    real_sum = real_sum + jnp.einsum(
        "scr,scn->crn", row_part[1], segment[1], preferred_element_type=jnp.float32
    )
    imag_sum = jnp.einsum(
        "scr,scn->crn", row_part[1], segment[0], preferred_element_type=jnp.float32
    )
    imag_sum = imag_sum - jnp.einsum(
        "scr,scn->crn", row_part[0], segment[1], preferred_element_type=jnp.float32
    )
    return jnp.stack([real_sum, imag_sum])


def local(voltages):
    in_rows, frames_dev, frame_len = voltages.shape
    dft_table = tap_table(frame_len, CH, FIRST, TAPS)
    columns_out = 2 * CH
    warmup = TAPS - 1
    frame_rows = voltages.reshape(in_rows * frames_dev, frame_len)
    own_taps = jnp.dot(frame_rows, dft_table, preferred_element_type=jnp.float32).reshape(
        in_rows, frames_dev, TAPS, columns_out
    )
    own_sum = own_taps[:, :, 0, :]
    for tap_idx in range(1, TAPS):
        own_sum = own_sum + jnp.pad(
            own_taps[:, : frames_dev - tap_idx, tap_idx, :], ((0, 0), (tap_idx, 0), (0, 0))
        )
    earlier = shifted(voltages, "tm", 1)
    earlier_taps = jnp.dot(
        earlier.reshape(in_rows * warmup, frame_len), dft_table, preferred_element_type=jnp.float32
    )
    carried = carry_terms(earlier_taps.reshape(in_rows, warmup, TAPS, columns_out), warmup)
    full_sum = own_sum + carried
    spectra = full_sum.astype(jnp.bfloat16)
    position = lax.axis_index("tm") * frames_dev + jnp.arange(frames_dev, dtype=jnp.int32)
    spectra = jnp.where((position >= warmup)[None, :, None], spectra, jnp.zeros_like(spectra))
    arranged = jnp.transpose(spectra.reshape(in_rows, frames_dev, 2, CH), (2, 1, 3, 0))
    turned = lax.all_to_all(arranged, "grp", split_axis=2, concat_axis=3, tiled=True)
    row_count = turned.shape[3] // lax.axis_size("tm")
    row_start = lax.axis_index("tm") * row_count
    visible = cross_terms(lax.all_gather(turned, "tm", axis=1, tiled=True), row_start, row_count)
    kept_count = frames_dev * lax.axis_size("tm") - warmup
    return visible * (1.0 / kept_count)


def solution(mesh):
    placed = (P("grp", "tm", None),)
    return jax.shard_map(
        local, mesh=mesh, in_specs=placed, out_specs=P(None, "grp", "tm", None), check_vma=False
    )
```

profile of v0, /device:TPU:0, one launch (start us, length us, event | category | flops | bytes accessed | tf_op | source)
XLA Modules:
  0.0 488.1 jit_solution(12623672119393750634)
XLA Ops:
  0.0 6.9 %collective-permute-start = (bf16[128,3,16384]{2,0,1:T(8,128)(2,1)}, bf16[128,3,16384]{2,0,1:T(8,128)(2,1)}, u32[]{:S(2)}, u32[]{:S(2)}) collective-permute-start(bf16[128,3,16384]{2,0,1:T(8,128)(2,1)} %param.1), channel_id=1, source_target_pairs={{0,1},{1,2},{2,3},{4,5},{5,6},{6,7},{8,9},{9,10},{10,11},{12,13},{... | collective-permute-start | bytes 37748744 | tf_op jit(solution)/shard_map/ppermute | solution.py:16
  10.7 18.9 %copy.32 = bf16[128,3,16384]{2,1,0:T(4,128)(2,1)} copy(bf16[128,3,16384]{2,0,1:T(8,128)(2,1)} %param.1) | data formatting | bytes 25165824 | tf_op args[0]
  29.6 19.3 %reshape.111 = bf16[384,16384]{1,0:T(8,128)(2,1)} reshape(bf16[128,3,16384]{2,1,0:T(4,128)(2,1)} %copy.32) | data formatting | bytes 25165824 | tf_op jit(solution)/shard_map/reshape | solution.py:71
  48.9 32.0 %fusion.6 = bf16[16384,1024]{1,0:T(8,128)(2,1)} fusion(s32[128]{0:T(128)S(1)} %iota_add_fusion, f32[16384]{0:T(1024)S(1)} %fusion.24), kind=kLoop, calls=%fused_computation.20 | loop fusion | flops 33554432 | bytes 4260352
  80.9 32.3 %fusion.7 = bf16[16384,1024]{1,0:T(8,128)(2,1)} fusion(bf16[16384,1024]{1,0:T(8,128)(2,1)} %fusion.6, f32[16384]{0:T(1024)S(1)} %fusion.34, s32[128]{0:T(128)S(1)} %iota_add_fusion), kind=kLoop, calls=%fused_computation.21 | loop fusion | flops 33554432 | bytes 4260352
  113.2 32.1 %fusion.8 = bf16[16384,1024]{1,0:T(8,128)(2,1)} fusion(bf16[16384,1024]{1,0:T(8,128)(2,1)} %fusion.7, f32[16384]{0:T(1024)S(1)} %fusion.26, s32[128]{0:T(128)S(1)} %iota_add_fusion), kind=kLoop, calls=%fused_computation.22 | loop fusion | flops 33554432 | bytes 4260352
  145.2 32.3 %fusion.9 = bf16[16384,1024]{1,0:T(8,128)(2,1)} fusion(bf16[16384,1024]{1,0:T(8,128)(2,1)} %fusion.8, f32[16384]{0:T(1024)S(1)} %fusion.33, s32[128]{0:T(128)S(1)} %iota_add_fusion), kind=kLoop, calls=%fused_computation.23 | loop fusion | flops 33554432 | bytes 4260352
  177.5 32.3 %fusion.10 = bf16[16384,1024]{1,0:T(8,128)(2,1)} fusion(bf16[16384,1024]{1,0:T(8,128)(2,1)} %fusion.9, f32[16384]{0:T(1024)S(1)} %fusion.28, s32[128]{0:T(128)S(1)} %iota_add_fusion), kind=kLoop, calls=%fused_computation.24 | loop fusion | flops 33554432 | bytes 4260352
  209.8 32.3 %fusion.11 = bf16[16384,1024]{1,0:T(8,128)(2,1)} fusion(bf16[16384,1024]{1,0:T(8,128)(2,1)} %fusion.10, f32[16384]{0:T(1024)S(1)} %fusion.32, s32[128]{0:T(128)S(1)} %iota_add_fusion), kind=kLoop, calls=%fused_computation.25 | loop fusion | flops 33554432 | bytes 4260352
  242.1 32.1 %fusion.12 = bf16[16384,1024]{1,0:T(8,128)(2,1)} fusion(bf16[16384,1024]{1,0:T(8,128)(2,1)} %fusion.11, f32[16384]{0:T(1024)S(1)} %fusion.30, s32[128]{0:T(128)S(1)} %iota_add_fusion), kind=kLoop, calls=%fused_computation.26 | loop fusion | flops 33554432 | bytes 4260352
  274.2 32.3 %fusion.13 = bf16[16384,1024]{1,0:T(8,128)(2,1)} fusion(bf16[16384,1024]{1,0:T(8,128)(2,1)} %fusion.12, f32[16384]{0:T(1024)S(1)} %fusion.31, s32[128]{0:T(128)S(1)} %iota_add_fusion), kind=kLoop, calls=%fused_computation.27 | loop fusion | flops 33554432 | bytes 4260352 | tf_op jit(solution)/shard_map/concatenate | solution.py:37
  306.5 22.9 %convolution_bitcast_fusion.1 = f32[384,1024]{0,1:T(8,128)} fusion(bf16[16384,1024]{1,0:T(8,128)(2,1)} %fusion.13, bf16[384,16384]{1,0:T(8,128)(2,1)S(1)} %bitcast.71), kind=kOutput, calls=%fused_computation.31 | convolution fusion | flops 12884901888 | bytes 47710208 | tf_op jit(solution)/shard_map/dot_general | solution.py:72
  329.4 1.9 copy.33
  332.6 0.8 copy.94
  333.4 18.7 %copy.36 = bf16[128,3,16384]{2,1,0:T(4,128)(2,1)} copy(bf16[128,3,16384]{2,0,1:T(8,128)(2,1)} %collective-permute-done) | data formatting | bytes 25165824 | tf_op jit(solution)/shard_map/ppermute | solution.py:16
  352.1 19.3 %reshape.113 = bf16[384,16384]{1,0:T(8,128)(2,1)} reshape(bf16[128,3,16384]{2,1,0:T(4,128)(2,1)} %copy.36) | data formatting | bytes 25165824 | tf_op jit(solution)/shard_map/reshape | solution.py:82
  371.4 25.0 %convolution_bitcast_fusion = f32[384,1024]{0,1:T(8,128)} fusion(bf16[16384,1024]{1,0:T(8,128)(2,1)} %fusion.13, bf16[384,16384]{1,0:T(8,128)(2,1)} %reshape.113), kind=kOutput, calls=%fused_computation.30 | convolution fusion | flops 12884901888 | bytes 47710208 | tf_op jit(solution)/shard_map/dot_general | solution.py:81
  396.5 1.9 copy.37
  398.3 1.9 reshape.114
  400.2 1.3 slice_bitcast_fusion
  401.5 1.5 slice.48
  403.0 1.8 slice.49
  405.0 1.5 broadcast_select_fusion
  406.7 0.9 copy.42
  407.6 6.7 %all-to-all-start = ((bf16[2,3,128,128]{3,0,1,2:T(2,128)(2,1)}), bf16[2,3,128,128]{3,0,1,2:T(2,128)(2,1)S(1)}, u32[]{:S(2)}, u32[]{:S(2)}) async-start(bf16[2,3,128,128]{3,0,1,2:T(2,128)(2,1)} %copy.42), calls=%async_computation | async-start | bytes 393216 | tf_op jit(solution)/shard_map/all_to_all | solution.py:90
  414.3 7.8 %all-to-all-done = bf16[2,3,128,128]{3,0,1,2:T(2,128)(2,1)S(1)} async-done(((bf16[2,3,128,128]{3,0,1,2:T(2,128)(2,1)}), bf16[2,3,128,128]{3,0,1,2:T(2,128)(2,1)S(1)}, u32[]{:S(2)}, u32[]{:S(2)}) %all-to-all-start) | async-done | bytes 196640 | tf_op jit(solution)/shard_map/all_to_all | solution.py:90
  422.2 7.4 %all_gather.3 = bf16[2,12,16,1024]{3,2,0,1:T(8,128)(2,1)S(1)} all-gather(bf16[2,3,16,1024]{3,2,0,1:T(8,128)(2,1)S(1)} %reshape.116), channel_id=1, replica_groups=mesh['grp'=8,'tm'=4] {'tm'}, dimensions={1}, use_global_device_ids=true | all-gather | bytes 983040 | tf_op jit(solution)/shard_map/all_gather | solution.py:93
  429.8 8.6 %fusion.17 = f32[16,256,1024]{2,1,0:T(8,128)} fusion(bf16[1,12,16,1024]{3,2,0,1:T(8,128)(2,1)S(1)} %get-tuple-element.8, bf16[1,12,16,256]{3,2,0,1:T(8,128)(2,1)S(1)} %get-tuple-element.5), kind=kOutput, calls=%fused_computation.35 | convolution fusion | flops 100663296 | bytes 17268736 | tf_op jit(solution)/shard_map/scr,scn->crn/dot_general | solution.py:51
  438.3 2.4 fusion.16
  440.7 14.1 %add_bitcast_fusion = f32[1,16,256,1024]{3,2,1,0:T(8,128)} fusion(f32[16,256,1024]{2,1,0:T(8,128)} %fusion.17, bf16[1,12,16,1024]{3,2,0,1:T(8,128)(2,1)S(1)} %get-tuple-element.7, bf16[1,12,16,256]{3,2,0,1:T(8,128)(2,1)S(1)} %get-tuple-element.6), kind=kOutput, calls=%fused_computation.2 | convolution fusion | flops 104857600 | bytes 34045952 | tf_op jit(solution)/shard_map/scr,scn->crn/dot_general | solution.py:54
  454.8 8.2 %subtract_bitcast_fusion = f32[1,16,256,1024]{3,2,1,0:T(8,128)} fusion(f32[16,256,1024]{2,1,0:T(8,128)S(1)} %fusion.16, bf16[1,12,16,1024]{3,2,0,1:T(8,128)(2,1)S(1)} %get-tuple-element.7, bf16[1,12,16,256]{3,2,0,1:T(8,128)(2,1)S(1)} %get-tuple-element.5), kind=kOutput, calls=%fused_computation.1 | convolution fusion | flops 104857600 | bytes 34045952 | tf_op jit(solution)/shard_map/scr,scn->crn/dot_general | solution.py:60
  463.0 24.9 %maximum_multiply_fusion = f32[2,16,256,1024]{3,2,1,0:T(8,128)} fusion(f32[1,16,256,1024]{3,2,1,0:T(8,128)} %subtract_bitcast_fusion, f32[1,16,256,1024]{3,2,1,0:T(8,128)} %add_bitcast_fusion), kind=kLoop, calls=%fused_computation | loop fusion | flops 16777216 | bytes 67108864 | tf_op jit(solution)/shard_map/mul | solution.py:95
  (28 shorter events, 5.6 us)
Async XLA Ops:
  0.0 333.4 %collective-permute-start = (bf16[128,3,16384]{2,0,1:T(8,128)(2,1)}, bf16[128,3,16384]{2,0,1:T(8,128)(2,1)}, u32[]{:S(2)}, u32[]{:S(2)}) collective-permute-start(bf16[128,3,16384]{2,0,1:T(8,128)(2,1)} %param.1), channel_id=1, source_target_pairs={{0,1},{1,2},{2,3},{4,5},{5,6},{6,7},{8,9},{9,10},{10,11},{12,13},{... | collective-permute-start | bytes 37748744 | tf_op jit(solution)/shard_map/ppermute | solution.py:16
  113.2 193.3 %slice-start = ((s8[12582912]{0:T(1024)(128)(4,1)}), s8[4194304]{0:T(1024)(128)(4,1)S(1)}, s32[]{:S(2)}) async-start(s8[12582912]{0:T(1024)(128)(4,1)} %bitcast.70), calls=%async_computation.1 | async-start | bytes 8388608
  177.5 129.0 %slice-start.1 = ((s8[12582912]{0:T(1024)(128)(4,1)}), s8[4194304]{0:T(1024)(128)(4,1)S(1)}, s32[]{:S(2)}) async-start(s8[12582912]{0:T(1024)(128)(4,1)} %bitcast.70), calls=%async_computation.2 | async-start | bytes 8388608
  242.1 64.4 %slice-start.2 = ((s8[12582912]{0:T(1024)(128)(4,1)}), s8[4194304]{0:T(1024)(128)(4,1)S(1)}, s32[]{:S(2)}) async-start(s8[12582912]{0:T(1024)(128)(4,1)} %bitcast.70), calls=%async_computation.3 | async-start | bytes 8388608
  407.6 14.4 %all-to-all-start = ((bf16[2,3,128,128]{3,0,1,2:T(2,128)(2,1)}), bf16[2,3,128,128]{3,0,1,2:T(2,128)(2,1)S(1)}, u32[]{:S(2)}, u32[]{:S(2)}) async-start(bf16[2,3,128,128]{3,0,1,2:T(2,128)(2,1)} %copy.42), calls=%async_computation | async-start | bytes 393216 | tf_op jit(solution)/shard_map/all_to_all | solution.py:90
where the time goes:
time: 493 us; the launch traced here: 488 us
  other arithmetic  288 us (58%)
  local copies, waits for them, and re-layouts  90.1 us (18%)
  matrix products  81.1 us (16%)
  starting transfers between devices  13.6 us (3%)
  waiting for transfers between devices  7.79 us (2%)
  blocking collectives  7.44 us (2%)
    unnamed x8, other arithmetic  225 us
    concatenate x1, other arithmetic, tap_table(): return jnp.concatenate(columns, axis=1).astype(jnp.bfloat16)  32.3 us
    dot_general x1, matrix products, local(): jnp.dot(earlier.reshape(in_rows * warmup, frame_len), dft_table, preferre...  25 us
    mul x1, other arithmetic, local(): return visible * (1.0 / kept_count)  24.9 us
    dot_general x1, matrix products, local(): jnp.dot(frame_rows, dft_table, preferred_element_type=jnp.float32)  22.9 us
    unnamed x9, local copies, waits for them, and re-layouts  19.9 us
    reshape x1, local copies, waits for them, and re-layouts, local(): frame_rows = voltages.reshape(in_rows * frames_dev, frame_len)  19.3 us
    reshape x1, local copies, waits for them, and re-layouts, local(): earlier.reshape(in_rows * warmup, frame_len)  19.3 us
  transfers between devices with their start and end apart: 2, of which 1 were waited for; matrix products, arithmetic and copies ran while one was open for 67% of the time, Pallas kernels for 0%

commit v1 on v0

v1 whole, which is shorter than its diff:
```python
import functools
import math

import jax
import jax.numpy as jnp
from jax import lax
from jax.experimental import pallas as pl
from jax.experimental.pallas import tpu as pltpu
from jax.sharding import PartitionSpec as P

CH = 128
TAPS = 4
FIRST = 2048
STEP = 128
CHUNK = 512
VMEM_LIMIT = 60 * 1024 * 1024


def phase_tables(frame_len):
    channel = FIRST + lax.broadcasted_iota(jnp.int32, (2, CH, STEP), 1)
    which = lax.broadcasted_iota(jnp.int32, (2, CH, STEP), 0)
    sample = lax.broadcasted_iota(jnp.int32, (2, CH, STEP), 2)
    index = jnp.where(which == 0, sample, STEP) * channel % frame_len
    angles = index.astype(jnp.float32) * jnp.float32(2.0 * math.pi / frame_len)
    return jnp.cos(angles), jnp.sin(angles)


def tap_windows(frame_len):
    shape = (frame_len // (2 * STEP), 2 * TAPS, STEP)
    row = lax.broadcasted_iota(jnp.int32, shape, 1)
    block = 2 * lax.broadcasted_iota(jnp.int32, shape, 0) + row // TAPS
    sample = block * STEP + lax.broadcasted_iota(jnp.int32, shape, 2)
    tap = row % TAPS
    offset = ((TAPS - 1 - tap) * frame_len + sample).astype(jnp.float32) + 0.5
    argument = offset / frame_len - TAPS / 2.0
    shape_part = jnp.sin(math.pi * argument) / (math.pi * argument)
    window = shape_part * (
        0.5 - 0.5 * jnp.cos(offset * jnp.float32(2.0 * math.pi / (TAPS * frame_len)))
    )
    return window * frame_len ** (-0.5)


def filter_kernel(v_ref, cos_ref, sin_ref, window_ref, own_ref, carry_ref, acc, even, odd, phase):
    step = pl.program_id(0)
    steps = pl.num_programs(0) - 1
    frames, in_rows, _ = v_ref.shape
    per_chunk = CHUNK // STEP

    def generate(table, chunk):
        cosine, sine = phase[0], phase[1]
        for part in range(per_chunk):
            window = window_ref[chunk * (per_chunk // 2) + part // 2]
            lanes = slice(part * STEP, (part + 1) * STEP)
            for k in range(TAPS):
                row = TAPS * (part % 2) + k
                scale = window[row : row + 1, :]
                at = 2 * CH * k
                table[at : at + CH, lanes] = (cosine * scale).astype(jnp.bfloat16)
                table[at + CH : at + 2 * CH, lanes] = (sine * -scale).astype(jnp.bfloat16)
            turn_cos, turn_sin = cos_ref[1], sin_ref[1]
            cosine, sine = cosine * turn_cos - sine * turn_sin, sine * turn_cos + cosine * turn_sin
        phase[0] = cosine
        phase[1] = sine

    def multiply(half, table):
        rows = v_ref[:, :, half * CHUNK : (half + 1) * CHUNK].reshape(frames * in_rows, CHUNK)
        acc[...] += lax.dot_general(
            rows, table[...], (((1,), (1,)), ((), ())), preferred_element_type=jnp.float32
        )

    @pl.when(step == 0)
    def _():
        acc[...] = jnp.zeros_like(acc)
        phase[0] = cos_ref[0]
        phase[1] = sin_ref[0]
        generate(even, 0)

    @pl.when(step < steps)
    def _():
        multiply(0, even)
        generate(odd, 2 * step + 1)
        multiply(1, odd)
        generate(even, jnp.minimum(2 * step + 2, 2 * steps - 1))

    @pl.when(step == steps)
    def _():
        warmup = TAPS - 1
        for f in range(frames + warmup):
            total = None
            for k in range(TAPS):
                if 0 <= f - k < frames:
                    piece = acc[(f - k) * in_rows : (f - k + 1) * in_rows, 2 * CH * k : 2 * CH * (k + 1)]
                    total = piece if total is None else total + piece
            turned = total.T
            if f < frames:
                own_ref[f] = turned.reshape(own_ref.shape[1:])
            else:
                carry_ref[f - frames] = turned.reshape(carry_ref.shape[1:])


def filter_bank(voltages, groups):
    in_rows, frames, frame_len = voltages.shape
    by_frame = jnp.transpose(voltages, (1, 0, 2))
    cosines, sines = phase_tables(frame_len)
    windows = tap_windows(frame_len)
    steps = frame_len // (2 * CHUNK)
    warmup = TAPS - 1
    tail = (2, groups, CH // groups, in_rows)
    whole = lambda x: pl.BlockSpec(x.shape, lambda i: (0,) * x.ndim)
    return pl.pallas_call(
        filter_kernel,
        grid=(steps + 1,),
        out_shape=(
            jax.ShapeDtypeStruct((frames, *tail), jnp.float32),
            jax.ShapeDtypeStruct((warmup, *tail), jnp.float32),
        ),
        in_specs=[
            pl.BlockSpec((frames, in_rows, 2 * CHUNK), lambda i: (0, 0, jnp.minimum(i, steps - 1))),
            whole(cosines),
            whole(sines),
            whole(windows),
        ],
        out_specs=(
            pl.BlockSpec((frames, *tail), lambda i: (0,) * 5),
            pl.BlockSpec((warmup, *tail), lambda i: (0,) * 5),
        ),
        scratch_shapes=[
            pltpu.VMEM((frames * in_rows, 2 * CH * TAPS), jnp.float32),
            pltpu.VMEM((2 * CH * TAPS, CHUNK), jnp.bfloat16),
            pltpu.VMEM((2 * CH * TAPS, CHUNK), jnp.bfloat16),
            pltpu.VMEM((2, CH, STEP), jnp.float32),
        ],
        compiler_params=pltpu.CompilerParams(vmem_limit_bytes=VMEM_LIMIT),
        name="filter_bank",
    )(by_frame, cosines, sines, windows)


def cross_kernel(depth, scale, spectra_ref, out_ref, right, left):
    channel = pl.program_id(0)
    times, groups, frames, _, channels, in_rows = spectra_ref.shape
    row_count = out_ref.shape[2]
    warmup = TAPS - 1
    halves, padded = right.shape[0], right.shape[1]

    @pl.when(channel == 0)
    def _():
        for half in range(halves):
            for g in range(groups):
                pieces = []
                for p in range(2):
                    for f in range(warmup, times * frames):
                        tile = spectra_ref[f // frames, g, f % frames, p].astype(jnp.float32)
                        pieces.append(tile[8 * half : 8 * half + 8])
                if padded > depth:
                    pieces.append(jnp.zeros((padded - depth, in_rows), jnp.float32))
                right[half, :, g * in_rows : (g + 1) * in_rows] = jnp.concatenate(pieces).astype(jnp.bfloat16)
            start = pl.multiple_of(lax.axis_index("tm") * row_count, 128)
            own = right[half, :, pl.ds(start, row_count)].astype(jnp.float32)
            left[half, 0] = own.T
            swapped = [own[depth // 2 : depth], -own[: depth // 2]]
            if padded > depth:
                swapped.append(own[depth:])
            left[half, 1] = jnp.concatenate(swapped).T

    half = channel // 8
    lane = lax.broadcasted_iota(jnp.int32, (row_count, padded), 1)
    chosen = lane % 8 == channel % 8
    for p in range(2):
        rows = jnp.where(chosen, left[half, p], 0.0).astype(jnp.bfloat16)
        out_ref[p, 0] = jnp.dot(rows, right[half], preferred_element_type=jnp.float32) * scale


def cross_multiply(spectra, row_count):
    times, groups, frames, _, channels, in_rows = spectra.shape
    kept = times * frames - (TAPS - 1)
    depth = 2 * kept * 8
    padded = -(-depth // 128) * 128
    halves = channels // 8
    return pl.pallas_call(
        functools.partial(cross_kernel, depth, 1.0 / kept),
        grid=(channels,),
        out_shape=jax.ShapeDtypeStruct((2, channels, row_count, groups * in_rows), jnp.float32),
        in_specs=[pl.BlockSpec(spectra.shape, lambda c: (0,) * 6)],
        out_specs=pl.BlockSpec((2, 1, row_count, groups * in_rows), lambda c: (0, c, 0, 0)),
        scratch_shapes=[
            pltpu.VMEM((halves, padded, groups * in_rows), jnp.bfloat16),
            pltpu.VMEM((halves, 2, row_count, padded), jnp.float32),
        ],
        compiler_params=pltpu.CompilerParams(vmem_limit_bytes=VMEM_LIMIT),
        name="cross_multiply",
    )(spectra)


def local(voltages):
    in_rows, frames, _ = voltages.shape
    groups, times = lax.axis_size("grp"), lax.axis_size("tm")
    own, carry = filter_bank(voltages, groups)
    carried = lax.ppermute(carry, "tm", [(i, i + 1) for i in range(times - 1)])
    first = own[: TAPS - 1] + carried
    spectra = jnp.concatenate([first, own[TAPS - 1 :]]).astype(jnp.bfloat16)
    turned = lax.all_to_all(spectra, "grp", split_axis=2, concat_axis=0)
    gathered = lax.all_gather(turned, "tm", axis=0)
    return cross_multiply(gathered, in_rows * groups // times)


def solution(mesh):
    return jax.shard_map(
        local,
        mesh=mesh,
        in_specs=(P("grp", "tm", None),),
        out_specs=P(None, "grp", "tm", None),
        check_vma=False,
    )
```

time: 493 us -> 76.1 us (0.15)
  other arithmetic: 288 us -> 5.02 us
  local copies, waits for them, and re-layouts: 90.1 us -> 0.01 us
  matrix products: 81.1 us -> 0 us
  Pallas kernels: 0 us -> 37.2 us
  blocking collectives: 7.44 us -> 29.3 us
  starting transfers between devices: 13.6 us -> 2.42 us
  waiting for transfers between devices: 7.79 us -> 1.52 us
    unnamed x8 -> x0, other arithmetic: 225 us -> none
    dot_general x6 -> x0, matrix products: 81.1 us -> none  [the longest x1 25 us: local(): jnp.dot(earlier.reshape(in_rows * warmup, frame_len), dft_table, preferre...]
    reshape x4 -> x0, local copies, waits for them, and re-layouts: 41.2 us -> none  [the longest x1 19.3 us: local(): frame_rows = voltages.reshape(in_rows * frames_dev, frame_len)]
    pallas_call x0 -> x2, Pallas kernels: none -> 37.2 us  [the longest x1 20.8 us: filter_bank(): pl.pallas_call(filter_kernel, grid=(steps + 1,), out_shape=(jax.ShapeDtyp...]
    concatenate x1 -> x0, other arithmetic: 32.3 us -> none  [tap_table(): return jnp.concatenate(columns, axis=1).astype(jnp.bfloat16)]
    mul x5 -> x2, other arithmetic: 26.8 us -> 2.65 us  [the longest x1 2.64 us: tap_windows(): return window * frame_len ** (-0.5)]
    unnamed x9 -> x0, local copies, waits for them, and re-layouts: 19.9 us -> none
    ppermute x1 -> x0, local copies, waits for them, and re-layouts: 18.7 us -> none  [shifted(): return lax.ppermute(x, axis, pairs)]
  transfers between devices with their start and end apart: 2 -> 1, of which waited for: 1 -> 1; matrix products, arithmetic and copies ran while one was open for 67% -> 0% of each run, Pallas kernels for 0% -> 0%
where the time goes in v1:
time: 76.1 us; the launch traced here: 75.5 us
  Pallas kernels  37.2 us (49%)
  blocking collectives  29.3 us (39%)
  other arithmetic  5.02 us (7%)
  starting transfers between devices  2.42 us (3%)
  waiting for transfers between devices  1.52 us (2%)
    pallas_call x1, Pallas kernels, filter_bank(): pl.pallas_call(filter_kernel, grid=(steps + 1,), out_shape=(jax.ShapeDtyp...  20.8 us
    pallas_call x1, Pallas kernels, cross_multiply(): pl.pallas_call(functools.partial(cross_kernel, depth, 1.0 / kept), grid=(...  16.3 us
    all_gather x1, blocking collectives, local(): gathered = lax.all_gather(turned, 'tm', axis=0)  15 us
    all_to_all x1, blocking collectives, local(): turned = lax.all_to_all(spectra, 'grp', split_axis=2, concat_axis=0)  14.2 us
    mul x1, other arithmetic, tap_windows(): return window * frame_len ** (-0.5)  2.64 us
    ppermute x1, starting transfers between devices, local(): carried = lax.ppermute(carry, 'tm', [(i, i + 1) for i in range(times - 1)])  2.42 us
  transfers between devices with their start and end apart: 1, of which 1 were waited for; matrix products, arithmetic and copies ran while one was open for 0% of the time, Pallas kernels for 0%

profile of v1, /device:TPU:0, one launch (start us, length us, event | category | flops | bytes accessed | tf_op | source)
XLA Modules:
  0.0 75.5 jit_solution(1857071621208195775)
XLA Ops:
  0.0 1.3 %fusion.6 = (f32[2,128,128]{2,1,0:T(8,128)}, f32[2,128,128]{2,1,0:T(8,128)}) fusion(s32[128]{0:T(128)S(1)} %iota_add_fusion, pred[2]{0:T(512)(128)(4,1)S(1)} %iota_compare_fusion), kind=kLoop, calls=%fused_computation.11 | loop fusion | flops 491520 | bytes 262658 | tf_op jit(solution)/shard_map/sin | solution.py:25
  1.3 2.6 %fusion.1.window_ref = f32[64,8,128]{2,1,0:T(8,128)} fusion(s32[8]{0:T(128)S(1)} %get-tuple-element.13, s32[8]{0:T(128)S(1)} %get-tuple-element.15, s32[64]{0:T(128)S(1)} %iota_multiply_fusion, s32[8]{0:T(128)S(1)} %get-tuple-element.14, s32[8]{0:T(128)S(1)} %get-tuple-element.16, pred[8]{0:T(512)(128)(4,1)S(1)} %get-tuple-element.11, ...), kind=kLoop, calls=%fused_computation.3 | loop fusion | flops 1245184 | bytes 262544 | tf_op jit(solution)/shard_map/mul | solution.py:40
  4.0 20.8 %filter_bank.1 = (f32[3,2,8,16,128]{4,3,2,1,0:T(8,128)}, f32[3,2,8,16,128]{4,3,2,1,0:T(8,128)}) custom-call(bf16[3,128,16384]{2,1,0:T(8,128)(2,1)} %bitcast.9, f32[2,128,128]{2,1,0:T(8,128)} %get-tuple-element.10.cos_ref, f32[2,128,128]{2,1,0:T(8,128)} %get-tuple-element.9.sin_ref, f32[64,8,128]{2,1,0:T(8,128)} %fusion.1.window_ref), custom_call_target="tpu_custom_call" | custom-call | tf_op jit(solution)/shard_map/filter_bank/pallas_call | solution.py:110
  24.8 2.4 %collective-permute-start = (f32[3,2,8,16,128]{4,3,2,1,0:T(8,128)}, f32[3,2,8,16,128]{4,3,2,1,0:T(8,128)S(1)}, u32[]{:S(2)}, u32[]{:S(2)}) collective-permute-start(f32[3,2,8,16,128]{4,3,2,1,0:T(8,128)} %get-tuple-element.8), channel_id=1, source_target_pairs={{0,1},{1,2},{2,3},{4,5},{5,6},{6,7},{8,9},{9,10},{10,11},{12,13},{... | collective-permute-start | bytes 1179656 | tf_op jit(solution)/shard_map/ppermute | solution.py:198
  27.3 1.5 %collective-permute-done = f32[3,2,8,16,128]{4,3,2,1,0:T(8,128)S(1)} collective-permute-done((f32[3,2,8,16,128]{4,3,2,1,0:T(8,128)}, f32[3,2,8,16,128]{4,3,2,1,0:T(8,128)S(1)}, u32[]{:S(2)}, u32[]{:S(2)}) %collective-permute-start) | collective-permute-done | bytes 393248 | tf_op jit(solution)/shard_map/ppermute | solution.py:198
  28.8 1.1 %fusion.2 = bf16[1,3,2,8,16,128]{5,4,3,2,1,0:T(8,128)(2,1)S(1)} fusion(f32[3,2,8,16,128]{4,3,2,1,0:T(8,128)} %get-tuple-element.7, f32[3,2,8,16,128]{4,3,2,1,0:T(8,128)S(1)} %collective-permute-done), kind=kLoop, calls=%fused_computation.4 | loop fusion | flops 196608 | bytes 983040 | tf_op jit(solution)/shard_map/broadcast_in_dim | solution.py:201
  29.9 14.2 %all_to_all.15 = bf16[1,3,2,8,16,128]{5,4,2,1,0,3:T(8,128)(2,1)S(1)} all-to-all(bf16[1,3,2,8,16,128]{5,4,2,1,0,3:T(8,128)(2,1)S(1)} %copy.4), channel_id=1, replica_groups=mesh['grp'=8,'tm'=4] {'grp'}, dimensions={3} | all-to-all | bytes 393216 | tf_op jit(solution)/shard_map/all_to_all | solution.py:201
  44.1 15.0 %all-gather = bf16[32,1,3,2,1,16,128]{6,5,4,3,2,1,0:T(8,128)(2,1)} all-gather(bf16[8,1,3,2,1,16,128]{6,5,4,3,2,1,0:T(8,128)(2,1)S(1)} %bitcast.11), channel_id=2, replica_groups=mesh['grp'=8,'tm'=4] {'tm'}, dimensions={0}, use_global_device_ids=true | all-gather | bytes 983040 | tf_op jit(solution)/shard_map/all_gather | solution.py:202
  59.1 16.3 %cross_multiply.1 = f32[2,16,256,1024]{3,2,1,0:T(8,128)} custom-call(bf16[4,8,3,2,16,128]{5,4,3,2,1,0:T(8,128)(2,1)} %bitcast.10), custom_call_target="tpu_custom_call" | custom-call | tf_op jit(solution)/shard_map/cross_multiply/pallas_call | solution.py:179
  (7 shorter events, 0.0 us)
Async XLA Ops:
  24.8 3.9 %collective-permute-start = (f32[3,2,8,16,128]{4,3,2,1,0:T(8,128)}, f32[3,2,8,16,128]{4,3,2,1,0:T(8,128)S(1)}, u32[]{:S(2)}, u32[]{:S(2)}) collective-permute-start(f32[3,2,8,16,128]{4,3,2,1,0:T(8,128)} %get-tuple-element.8), channel_id=1, source_target_pairs={{0,1},{1,2},{2,3},{4,5},{5,6},{6,7},{8,9},{9,10},{10,11},{12,13},{... | collective-permute-start | bytes 1179656 | tf_op jit(solution)/shard_map/ppermute | solution.py:198

commit v2 on v1

--- a/solution.py
+++ b/solution.py
@@ -95,7 +95,7 @@
             if f < frames:
                 own_ref[f] = turned.reshape(own_ref.shape[1:])
             else:
-                carry_ref[f - frames] = turned.reshape(carry_ref.shape[1:])
+                carry_ref[f - frames] = turned.reshape(carry_ref.shape[1:]).astype(jnp.bfloat16)
 
 
 def filter_bank(voltages, groups):
@@ -112,7 +112,7 @@
         grid=(steps + 1,),
         out_shape=(
             jax.ShapeDtypeStruct((frames, *tail), jnp.float32),
-            jax.ShapeDtypeStruct((warmup, *tail), jnp.float32),
+            jax.ShapeDtypeStruct((warmup, *tail), jnp.bfloat16),
         ),
         in_specs=[
             pl.BlockSpec((frames, in_rows, 2 * CHUNK), lambda i: (0, 0, jnp.minimum(i, steps - 1))),
@@ -191,16 +191,165 @@
     )(spectra)
 
 
+def spread_kernel(
+    own_ref, carry_ref, out_ref, carried, send, local_sem, carry_sems, group_sems, partner_sems, row_sems, relay_sems
+):
+    frames, _, groups = own_ref.shape[:3]
+    times = out_ref.shape[0]
+    pairs = times // 2
+    warmup = TAPS - 1
+    unused = warmup // frames
+    g, t = lax.axis_index("grp"), lax.axis_index("tm")
+    partner = t + 1 - 2 * lax.rem(t, 2)
+
+    def copy(src, dst, sems, at, device):
+        return pltpu.make_async_remote_copy(
+            src_ref=src,
+            dst_ref=dst,
+            send_sem=sems.at[(0, *at)],
+            recv_sem=sems.at[(1, *at)],
+            device_id=device,
+            device_id_type=pl.DeviceIdType.MESH,
+        )
+
+    barrier = pltpu.get_barrier_semaphore()
+    for d in range(1, groups):
+        pl.semaphore_signal(
+            barrier, inc=1, device_id=(lax.rem(g + d, groups), t), device_id_type=pl.DeviceIdType.MESH
+        )
+    for d in range(1, times):
+        pl.semaphore_signal(
+            barrier, inc=1, device_id=(g, lax.rem(t + d, times)), device_id_type=pl.DeviceIdType.MESH
+        )
+    pl.semaphore_wait(barrier, groups + times - 2)
+
+    carry_copy = copy(carry_ref, carried, carry_sems, (), (g, lax.rem(t + 1, times)))
+
+    @pl.when(t < times - 1)
+    def _():
+        carry_copy.start()
+
+    @pl.when(t > 0)
+    def _():
+        carry_copy.wait_recv()
+
+    @pl.when(t == 0)
+    def _():
+        carried[...] = jnp.zeros_like(carried)
+
+    for f in range(frames):
+        for p in range(2):
+            total = own_ref[f, p]
+            if f < warmup:
+                total = total + carried[f, p].astype(jnp.float32)
+            send[:, f, p] = total.astype(jnp.bfloat16)
+    keep = pltpu.make_async_copy(send.at[g], out_ref.at[t, g], local_sem)
+    keep.start()
+    keep.wait()
+
+    def source(d):
+        return lax.rem(g + groups - d, groups)
+
+    def other(at, e):
+        return lax.rem(at + times - 2 * e, times)
+
+    def to_group(d):
+        to = lax.rem(g + d, groups)
+        return copy(send.at[to], out_ref.at[t, g], group_sems, (d,), (to, t))
+
+    def to_partner(d):
+        block = out_ref.at[t, source(d)]
+        return copy(block, block, partner_sems, (d,), (g, partner))
+
+    def to_row(e, d):
+        block = out_ref.at[t, source(d)]
+        return copy(block, block, row_sems, (e, d), (g, lax.rem(t + 2 * e, times)))
+
+    def relayed(e, d):
+        block = out_ref.at[other(t, e), source(d)]
+        return copy(block, block, relay_sems, (e, d), (g, partner))
+
+    @pl.when(t >= unused)
+    def _():
+        for d in range(1, groups):
+            to_group(d).start()
+        for d in range(groups):
+            if d:
+                to_group(d).wait_recv()
+            for e in range(1, pairs):
+                to_row(e, d).start()
+            to_partner(d).start()
+
+    for e in range(1, pairs):
+
+        @pl.when(other(t, e) >= unused)
+        def _(e=e):
+            for d in range(groups):
+                to_row(e, d).wait_recv()
+                relayed(e, d).start()
+
+    @pl.when(partner >= unused)
+    def _():
+        for d in range(groups):
+            to_partner(d).wait_recv()
+
+    for e in range(1, pairs):
+
+        @pl.when(other(partner, e) >= unused)
+        def _(e=e):
+            for d in range(groups):
+                relayed(e, d).wait_recv()
+
+        @pl.when(other(t, e) >= unused)
+        def _(e=e):
+            for d in range(groups):
+                relayed(e, d).wait_send()
+
+    @pl.when(t >= unused)
+    def _():
+        for d in range(groups):
+            if d:
+                to_group(d).wait_send()
+            to_partner(d).wait_send()
+            for e in range(1, pairs):
+                to_row(e, d).wait_send()
+
+    @pl.when(t < times - 1)
+    def _():
+        carry_copy.wait_send()
+
+
+def spread(own, carry):
+    frames, parts, groups, channels, in_rows = own.shape
+    times = lax.axis_size("tm")
+    vmem = pl.BlockSpec(memory_space=pltpu.VMEM)
+    return pl.pallas_call(
+        spread_kernel,
+        out_shape=jax.ShapeDtypeStruct((times, groups, frames, parts, channels, in_rows), jnp.bfloat16),
+        in_specs=[vmem, vmem],
+        out_specs=vmem,
+        scratch_shapes=[
+            pltpu.VMEM(carry.shape, carry.dtype),
+            pltpu.VMEM((groups, frames, parts, channels, in_rows), jnp.bfloat16),
+            pltpu.SemaphoreType.DMA,
+            pltpu.SemaphoreType.DMA((2,)),
+            pltpu.SemaphoreType.DMA((2, groups)),
+            pltpu.SemaphoreType.DMA((2, groups)),
+            pltpu.SemaphoreType.DMA((2, times // 2, groups)),
+            pltpu.SemaphoreType.DMA((2, times // 2, groups)),
+        ],
+        compiler_params=pltpu.CompilerParams(
+            collective_id=0, has_side_effects=True, vmem_limit_bytes=VMEM_LIMIT
+        ),
+        name="spread",
+    )(own, carry)
+
+
 def local(voltages):
-    in_rows, frames, _ = voltages.shape
+    in_rows, _, _ = voltages.shape
     groups, times = lax.axis_size("grp"), lax.axis_size("tm")
     own, carry = filter_bank(voltages, groups)
-    carried = lax.ppermute(carry, "tm", [(i, i + 1) for i in range(times - 1)])
-    first = own[: TAPS - 1] + carried
-    spectra = jnp.concatenate([first, own[TAPS - 1 :]]).astype(jnp.bfloat16)
-    turned = lax.all_to_all(spectra, "grp", split_axis=2, concat_axis=0)
-    gathered = lax.all_gather(turned, "tm", axis=0)
-    return cross_multiply(gathered, in_rows * groups // times)
+    return cross_multiply(spread(own, carry), in_rows * groups // times)
 
 
 def solution(mesh):

time: 76.1 us -> 63.4 us (0.83)
  blocking collectives: 29.3 us -> 0 us
  Pallas kernels: 37.2 us -> 58.7 us
  starting transfers between devices: 2.42 us -> 0 us
  waiting for transfers between devices: 1.52 us -> 0 us
  other arithmetic: 5.02 us -> 3.96 us
    pallas_call x0 -> x1, Pallas kernels: none -> 21.6 us  [spread(): pl.pallas_call(spread_kernel, out_shape=jax.ShapeDtypeStruct((times, grou...]
    all_gather x1 -> x0, blocking collectives: 15 us -> none  [local(): gathered = lax.all_gather(turned, 'tm', axis=0)]
    all_to_all x1 -> x0, blocking collectives: 14.2 us -> none  [local(): turned = lax.all_to_all(spectra, 'grp', split_axis=2, concat_axis=0)]
    ppermute x1 -> x0, starting transfers between devices: 2.42 us -> none  [local(): carried = lax.ppermute(carry, 'tm', [(i, i + 1) for i in range(times - 1)])]
    ppermute x1 -> x0, waiting for transfers between devices: 1.52 us -> none  [local(): carried = lax.ppermute(carry, 'tm', [(i, i + 1) for i in range(times - 1)])]
    broadcast_in_dim x1 -> x0, other arithmetic: 1.05 us -> none  [local(): turned = lax.all_to_all(spectra, 'grp', split_axis=2, concat_axis=0)]
  transfers between devices with their start and end apart: 1 -> 0, of which waited for: 1 -> 0; matrix products, arithmetic and copies ran while one was open for 0% -> 0% of each run, Pallas kernels for 0% -> 0%
where the time goes in v2:
time: 63.4 us; the launch traced here: 62.7 us
  Pallas kernels  58.7 us (93%)
  other arithmetic  3.96 us (6%)
    pallas_call x1, Pallas kernels, spread(): pl.pallas_call(spread_kernel, out_shape=jax.ShapeDtypeStruct((times, grou...  21.6 us
    pallas_call x1, Pallas kernels, filter_bank(): pl.pallas_call(filter_kernel, grid=(steps + 1,), out_shape=(jax.ShapeDtyp...  20.8 us
    pallas_call x1, Pallas kernels, cross_multiply(): pl.pallas_call(functools.partial(cross_kernel, depth, 1.0 / kept), grid=(...  16.4 us
    mul x1, other arithmetic, tap_windows(): return window * frame_len ** (-0.5)  2.64 us
    sin x1, other arithmetic, phase_tables(): return (jnp.cos(angles), jnp.sin(angles))  1.3 us

profile of v2, /device:TPU:0, one launch (start us, length us, event | category | flops | bytes accessed | tf_op | source)
XLA Modules:
  0.0 62.7 jit_solution(18174354249770302430)
XLA Ops:
  0.0 2.6 %fusion.1.window_ref = f32[64,8,128]{2,1,0:T(8,128)} fusion(s32[8]{0:T(128)S(1)} %get-tuple-element.13, s32[8]{0:T(128)S(1)} %get-tuple-element.15, s32[64]{0:T(128)S(1)} %iota_multiply_fusion, s32[8]{0:T(128)S(1)} %get-tuple-element.14, s32[8]{0:T(128)S(1)} %get-tuple-element.16, pred[8]{0:T(512)(128)(4,1)S(1)} %get-tuple-element.11, ...), kind=kLoop, calls=%fused_computation.2 | loop fusion | flops 1245184 | bytes 262544 | tf_op jit(solution)/shard_map/mul | solution.py:40
  2.7 1.3 %fusion.5 = (f32[2,128,128]{2,1,0:T(8,128)}, f32[2,128,128]{2,1,0:T(8,128)}) fusion(s32[128]{0:T(128)S(1)} %iota_add_fusion, pred[2]{0:T(512)(128)(4,1)S(1)} %iota_compare_fusion), kind=kLoop, calls=%fused_computation.9 | loop fusion | flops 491520 | bytes 262658 | tf_op jit(solution)/shard_map/sin | solution.py:25
  4.0 20.8 %filter_bank.1 = (f32[3,2,8,16,128]{4,3,2,1,0:T(8,128)}, bf16[3,2,8,16,128]{4,3,2,1,0:T(8,128)(2,1)}) custom-call(bf16[3,128,16384]{2,1,0:T(8,128)(2,1)} %bitcast.1, f32[2,128,128]{2,1,0:T(8,128)} %get-tuple-element.10.cos_ref, f32[2,128,128]{2,1,0:T(8,128)} %get-tuple-element.9.sin_ref, f32[64,8,128]{2,1,0:T(8,128)} %fusion.1.window_ref), custom_call_target="tpu_custom_call" | custom-call | tf_op jit(solution)/shard_map/filter_bank/pallas_call | solution.py:110
  24.7 21.6 %spread.1.spectra_ref = bf16[4,8,3,2,16,128]{5,4,3,2,1,0:T(8,128)(2,1)} custom-call(f32[3,2,8,16,128]{4,3,2,1,0:T(8,128)} %get-tuple-element.7.own_ref, bf16[3,2,8,16,128]{4,3,2,1,0:T(8,128)(2,1)} %get-tuple-element.8.carry_ref), custom_call_target="tpu_custom_call" | custom-call | tf_op jit(solution)/shard_map/spread/pallas_call | solution.py:326
  46.3 16.4 %cross_multiply.1 = f32[2,16,256,1024]{3,2,1,0:T(8,128)} custom-call(bf16[4,8,3,2,16,128]{5,4,3,2,1,0:T(8,128)(2,1)} %spread.1.spectra_ref), custom_call_target="tpu_custom_call" | custom-call | tf_op jit(solution)/shard_map/cross_multiply/pallas_call | solution.py:179
  (6 shorter events, 0.0 us)
